TPU v7x, 128 devices: a whole 4x4x4 slice. The times are simulated.
128 devices in a mesh: tensor: 8 (over z, core), fsdp: 16 (over x, y).
Axes of the slice: x: 4, y: 4, z: 4, core: 2. Of those that a mesh axis runs over, the one named last changes fastest.
Arguments:
- momentum: float32 [4096, 28672], P('tensor', 'fsdp'), may hold values from -6 to 6
- gradient: bfloat16 [4096, 28672], P('tensor', 'fsdp'), may hold values from -6 to 6
- right_factor: float32 [28672, 512], P('fsdp'), may hold values from -0.03125 to 0.03125
Outputs:
- new_momentum: float32 [4096, 28672], P('tensor', 'fsdp')
- update: float32 [4096, 28672], P('tensor', 'fsdp')
- new_right: float32 [28672, 512], P('fsdp')
All inputs are finite; a program needn't handle non-finite values.
Results may differ from a plain program's by a relative error of at most 0.0003.
Values sent between devices are 32-bit elements; how exact they have to be, the bound alone decides.
A program may use at most 128 MiB of HBM per device.

v0:
```python
import functools
import jax
import jax.numpy as jnp
from jax import lax
from jax.sharding import Mesh
from jax.sharding import PartitionSpec as P

ROWS = 4096
COLS = 28672
RANK = 512
FSDP = ("fsdp_0", "fsdp_1")
TENSOR = ("tensor_0", "tensor_1")
TENSOR_FSDP = ("tensor_0", "tensor_1", "fsdp_0", "fsdp_1")


def total_of_pieces(value, axis):
    parts = lax.all_gather(value, axis)
    return parts.sum(axis=0)


def in_blocks(value, dim, devices):
    lengths = value.shape
    parts = value.reshape(*lengths[:dim], devices, lengths[dim] // devices, *lengths[dim + 1 :])
    return jnp.moveaxis(parts, dim, 0)


def sum_at_owner(value, axis, dim):
    devices = lax.axis_size(axis)
    parts = lax.all_to_all(in_blocks(value, dim, devices), axis, 0, 0, tiled=True)
    return jnp.sum(parts, axis=0)


def over_axes(value, axes):
    return functools.reduce(lax.psum, axes, value)


def inner_rows(first, second):
    return lax.dot_general(
        first,
        second,
        (((0,), (0,)), ((), ())),
        precision=lax.Precision.HIGHEST,
        preferred_element_type=jnp.float32,
    )


def outer_rank(first, second):
    return lax.dot_general(
        first,
        second,
        (((1,), (1,)), ((), ())),
        precision=lax.Precision.HIGHEST,
        preferred_element_type=jnp.float32,
    )


def orthonormal(block, gram):
    lower = jnp.linalg.cholesky(gram)
    return jax.scipy.linalg.solve_triangular(lower, block.T, lower=True).T


def per_device(momentum, gradient, right_factor):
    buffer = momentum + gradient.astype(jnp.float32)
    partial_value = jnp.dot(
        buffer, right_factor, precision=lax.Precision.HIGHEST, preferred_element_type=jnp.float32
    )
    left = lax.psum(partial_value, FSDP)
    gram = total_of_pieces(inner_rows(left, left), TENSOR)
    ortho = orthonormal(left, gram)
    right_part = inner_rows(buffer, ortho)
    right_block = sum_at_owner(right_part, TENSOR, 0)
    colsq = over_axes(jnp.sum(right_block * right_block, axis=0), TENSOR_FSDP)
    right = lax.all_gather(right_block, TENSOR, axis=0, tiled=True)
    normed = right / jnp.sqrt(colsq + 1e-06)
    new_momentum = buffer - 0.05 * outer_rank(ortho, right)
    scale = jnp.sqrt(jnp.float32(ROWS * COLS / RANK))
    update = scale * outer_rank(ortho, normed)
    return (new_momentum, update, normed)


def solution(mesh):
    finer = Mesh(mesh.devices.reshape(4, 2, 4, 4), ("tensor_0", "tensor_1", "fsdp_0", "fsdp_1"))
    placed = (P(TENSOR, FSDP), P(TENSOR, FSDP), P(FSDP, None))
    return jax.shard_map(
        per_device,
        mesh=finer,
        in_specs=placed,
        out_specs=(P(TENSOR, FSDP), P(TENSOR, FSDP), P(FSDP, None)),
        check_vma=False,
    )
```

profile of v0, /device:TPU:0, one launch (start us, length us, event | category | flops | bytes accessed | tf_op | source)
XLA Modules:
  0.0 453.6 jit_solution(2981976357336586488)
XLA Ops:
  7.2 10.3 %fusion.1 = f32[512,512]{1,0:T(8,128)} fusion(f32[1792,512]{1,0:T(8,128)} %param.5, f32[512,1792]{1,0:T(8,128)} %param.3, bf16[512,1792]{1,0:T(8,128)(2,1)} %param.4), kind=kOutput, calls=%fused_computation.7 | convolution fusion | flops 5638979584 | bytes 10223616 | tf_op jit(solution)/shard_map/dot_general | solution.py:64
  17.6 89.8 %all-reduce.3.cloned.1.call-done = f32[512,512]{1,0:T(8,128)} async-done(((f32[512,512]{1,0:T(8,128)}), f32[512,512]{1,0:T(8,128)}) %all-reduce.3.cloned.1.call-update) | async-done | bytes 1048592 | tf_op jit(solution)/shard_map/psum | solution.py:67
  107.4 4.5 %fusion.36 = f32[512,512]{1,0:T(8,128)} fusion(f32[512,512]{1,0:T(8,128)} %all-reduce.3.cloned.1.call-done), kind=kOutput, calls=%fused_computation.78 | convolution fusion | flops 1610612736 | bytes 2097152 | tf_op jit(solution)/shard_map/dot_general | solution.py:38
  112.5 48.7 %all-gather.6.cloned.1.call-done = f32[4096,512]{1,0:T(8,128)} async-done(((f32[512,512]{1,0:T(8,128)}), f32[4096,512]{1,0:T(8,128)}) %all-gather.6.cloned.1.call-update) | async-done | bytes 8388624 | tf_op jit(solution)/shard_map/all_gather | solution.py:17
  161.2 4.5 reduce_sum.27
  166.3 1.0 copy-done.8
  167.3 11.7 %cholesky.104 = f32[128,128]{1,0:T(8,128)S(1)} custom-call(f32[128,128]{1,0:T(8,128)S(1)} %cholesky.266), custom_call_target="Cholesky" | custom-call | tf_op jit(solution)/shard_map/jit(cholesky)/cholesky | solution.py:58
  179.1 9.8 %custom-call.31 = f32[1,128,128]{1,2,0:T(8,128)S(1)} custom-call(f32[1,128,128]{2,1,0:T(8,128)S(1)} %get-tuple-element.30), custom_call_target="InvertDiagBlocksLowerTriangular" | custom-call | tf_op jit(solution)/shard_map/jit(cholesky)/cholesky | solution.py:58
  189.0 1.2 constant_dynamic-update-slice_fusion.3
  190.2 1.3 convolution_subtract_fusion.3
  191.5 11.9 %cholesky.217 = f32[128,128]{1,0:T(8,128)S(1)} custom-call(f32[128,128]{1,0:T(8,128)S(1)} %cholesky.270), custom_call_target="Cholesky" | custom-call | tf_op jit(solution)/shard_map/jit(cholesky)/cholesky | solution.py:58
  203.4 9.8 %custom-call.32 = f32[1,128,128]{1,2,0:T(8,128)S(1)} custom-call(f32[1,128,128]{2,1,0:T(8,128)S(1)} %get-tuple-element.27), custom_call_target="InvertDiagBlocksLowerTriangular" | custom-call | tf_op jit(solution)/shard_map/jit(cholesky)/cholesky | solution.py:58
  213.5 1.3 convolution_subtract_fusion.4
  214.8 11.7 %cholesky.238 = f32[128,128]{1,0:T(8,128)S(1)} custom-call(f32[128,128]{1,0:T(8,128)S(1)} %cholesky.275), custom_call_target="Cholesky" | custom-call | tf_op jit(solution)/shard_map/jit(cholesky)/cholesky | solution.py:58
  226.5 0.7 compare_reduce_fusion.1
  227.3 9.8 %custom-call.33 = f32[1,128,128]{1,2,0:T(8,128)S(1)} custom-call(f32[1,128,128]{2,1,0:T(8,128)S(1)} %get-tuple-element.24), custom_call_target="InvertDiagBlocksLowerTriangular" | custom-call | tf_op jit(solution)/shard_map/jit(cholesky)/cholesky | solution.py:58
  237.3 1.2 convolution_subtract_fusion.5
  238.5 12.1 %cholesky.255 = f32[128,128]{1,0:T(8,128)S(1)} custom-call(f32[128,128]{1,0:T(8,128)S(1)} %convolution_subtract_fusion.5), custom_call_target="Cholesky" | custom-call | tf_op jit(solution)/shard_map/jit(cholesky)/cholesky | solution.py:58
  250.7 0.6 compare_reduce_fusion
  251.3 0.7 compare_reduce_fusion.2
  254.5 1.1 select_select_fusion
  255.6 14.2 %while.1 = (s32[]{:T(128)}, f32[512,512]{1,0:T(8,128)}, s32[4,2]{0,1:T(2,128)S(1)}, f32[4,128,128]{2,1,0:T(8,128)}, s32[]{:T(128)}) while((s32[]{:T(128)}, f32[512,512]{1,0:T(8,128)}, s32[4,2]{0,1:T(2,128)S(1)}, f32[4,128,128]{2,1,0:T(8,128)}, s32[]{:T(128)}) %tuple.31), condition=%wide.while_cond, body=%wide.while_body.sunk | while | flops 2 | bytes 132205 | solution.py:59
  255.7 0.6 fusion.48
  256.3 2.9 bitcast_dynamic-update-slice_fusion.2
  259.2 0.6 fusion.48
  259.8 2.9 bitcast_dynamic-update-slice_fusion.2
  262.8 0.6 fusion.48
  263.4 2.9 bitcast_dynamic-update-slice_fusion.2
  266.3 0.6 fusion.48
  266.9 2.8 bitcast_dynamic-update-slice_fusion.2
  269.8 40.1 %custom-call.34 = f32[4,128,128]{1,2,0:T(8,128)S(1)} custom-call(f32[4,128,128]{2,1,0:T(8,128)} %get-tuple-element.10), custom_call_target="InvertDiagBlocksLowerTriangular" | custom-call | tf_op jit(solution)/shard_map/jit(_solve_triangular)/triangular_solve | solution.py:59
  310.6 1.9 convolution_subtract_fusion.1
  312.5 1.3 fusion.24
  313.7 1.9 convolution_subtract_fusion
  315.6 1.3 fusion.22
  316.9 2.5 convolution_subtract_fusion.2
  319.4 1.3 fusion.21
  320.7 12.3 %fusion = f32[1792,512]{1,0:T(8,128)S(1)} fusion(f32[512,1792]{1,0:T(8,128)S(1)} %copy-done, bf16[512,1792]{1,0:T(8,128)(2,1)S(1)} %copy-done.2, f32[128,512]{1,0:T(8,128)S(1)} %fusion.21, f32[128,512]{1,0:T(8,128)S(1)} %fusion.22, f32[128,512]{1,0:T(8,128)S(1)} %fusion.24, f32[128,512]{1,0:T(8,128)S(1)} %fusion.11), kind=kOutput, calls=%fused_computation.6 | convolution fusion | flops 5639766016 | bytes 10223616 | tf_op jit(solution)/shard_map/dot_general | solution.py:38
  333.0 47.3 %all_to_all.5 = f32[8,224,512]{2,1,0:T(8,128)} all-to-all(f32[8,224,512]{2,1,0:T(8,128)S(1)} %bitcast.56), channel_id=1, replica_groups=mesh['tensor_0'=4,'tensor_1'=2,'fsdp_0'=4,'fsdp_1'=4] {'tensor_0','tenso..., dimensions={0} | all-to-all | bytes 7340032 | tf_op jit(solution)/shard_map/all_to_all | solution.py:29
  380.3 3.3 reduce_sum.28
  383.6 1.1 multiply_reduce_fusion
  384.6 8.9 %psum.36 = f32[512]{0:T(512)S(1)} all-reduce(f32[512]{0:T(512)S(1)} %multiply_reduce_fusion), channel_id=1, replica_groups=mesh['tensor_0'=4,'tensor_1'=2,'fsdp_0'=4,'fsdp_1'=4] {'tensor_0'}, use_global_device_ids=true, to_apply=%region_12.13 | all-reduce | flops 512 | bytes 4096 | tf_op jit(solution)/shard_map/psum | solution.py:34
  393.5 2.5 psum.37
  396.0 10.4 %psum.38 = f32[512]{0:T(512)S(1)} all-reduce(f32[512]{0:T(512)S(1)} %psum.37), channel_id=1, replica_groups=mesh['tensor_0'=4,'tensor_1'=2,'fsdp_0'=4,'fsdp_1'=4] {'fsdp_0'}, use_global_device_ids=true, to_apply=%region_14.15 | all-reduce | flops 512 | bytes 4096 | tf_op jit(solution)/shard_map/psum | solution.py:34
  406.4 10.5 %psum.39 = f32[512]{0:T(512)S(1)} all-reduce(f32[512]{0:T(512)S(1)} %psum.38), channel_id=1, replica_groups=mesh['tensor_0'=4,'tensor_1'=2,'fsdp_0'=4,'fsdp_1'=4] {'fsdp_1'}, use_global_device_ids=true, to_apply=%region_15.16 | all-reduce | flops 512 | bytes 4096 | tf_op jit(solution)/shard_map/psum | solution.py:34
  416.9 2.5 broadcast_divide_fusion
  419.5 13.7 %convolution_multiply_fusion = f32[512,1792]{1,0:T(8,128)} fusion(f32[1792,512]{1,0:T(8,128)S(1)} %broadcast_divide_fusion, f32[128,512]{1,0:T(8,128)S(1)} %fusion.21, f32[128,512]{1,0:T(8,128)S(1)} %copy-done.7, f32[128,512]{1,0:T(8,128)S(1)} %fusion.24, f32[128,512]{1,0:T(8,128)S(1)} %fusion.11), kind=kOutput, calls=%fused_computation.4 | convolution fusion | flops 5638848512 | bytes 8388608 | tf_op jit(solution)/shard_map/dot_general | solution.py:48
  433.2 13.7 %multiply_subtract_fusion = f32[512,1792]{1,0:T(8,128)} fusion(f32[1792,512]{1,0:T(8,128)S(1)} %copy-done.4, f32[512,1792]{1,0:T(8,128)S(1)} %copy-done.1, bf16[512,1792]{1,0:T(8,128)(2,1)S(1)} %copy-done.2, f32[128,512]{1,0:T(8,128)S(1)} %fusion.21, f32[128,512]{1,0:T(8,128)S(1)} %copy-done.7, f32[128,512]{1,0:T(8,128)S(1)} %fusion.24, ...), kind=kOutput, calls=%fused_computation.2 | convolution fusion | flops 5641601024 | bytes 13893632 | tf_op jit(solution)/shard_map/dot_general | solution.py:48
  (47 shorter events, 3.0 us)
Async XLA Ops:
  7.2 100.2 %all-reduce.3.cloned.1.call-start = ((), (), s32[]{:S(2)}) async-start(), calls=%async_computation.1 | async-start | bytes 2097152 | tf_op jit(solution)/shard_map/psum | solution.py:67
  17.6 143.6 %all-gather.6.cloned.1.call-start = ((), (), s32[]{:S(2)}) async-start(), calls=%async_computation.3 | async-start | bytes 9437184 | tf_op jit(solution)/shard_map/all_gather | solution.py:17
  112.0 304.9 %all-gather.4.cloned.1.call-start = ((), (), s32[]{:S(2)}) async-start(), calls=%async_computation.2 | async-start | bytes 4128768 | tf_op jit(solution)/shard_map/all_gather | solution.py:73
  166.3 1.0 copy-start.8
  179.0 130.9 %copy-start.5 = (f32[512,512]{1,0:T(8,128)S(1)}, f32[512,512]{1,0:T(8,128)}, u32[]{:S(2)}) copy-start(f32[512,512]{1,0:T(8,128)} %all-reduce.3.cloned.1.call-done) | copy-start | bytes 3145732
  255.6 65.1 %copy-start.2 = (bf16[512,1792]{1,0:T(8,128)(2,1)S(1)}, bf16[512,1792]{1,0:T(8,128)(2,1)}, u32[]{:S(2)}) copy-start(bf16[512,1792]{1,0:T(8,128)(2,1)} %param.4) | copy-start | bytes 5505028
  309.9 0.7 copy-start.9
  309.9 10.8 %copy-start = (f32[512,1792]{1,0:T(8,128)S(1)}, f32[512,1792]{1,0:T(8,128)}, u32[]{:S(2)}) copy-start(f32[512,1792]{1,0:T(8,128)} %param.3) | copy-start | bytes 11010052
  316.9 16.1 %copy-start.6 = (f32[128,512]{1,0:T(8,128)}, f32[128,512]{1,0:T(8,128)S(1)}, u32[]{:S(2)}) copy-start(f32[128,512]{1,0:T(8,128)S(1)} %fusion.22) | copy-start | bytes 786436
  416.8 2.6 copy-start.7
  419.4 13.7 %copy-start.3 = (f32[1792,512]{1,0:T(8,128)}, f32[1792,512]{1,0:T(8,128)S(1)}, u32[]{:S(2)}) copy-start(f32[1792,512]{1,0:T(8,128)S(1)} %broadcast_divide_fusion) | copy-start | bytes 11010052
  419.4 13.7 %copy-start.1 = (f32[512,1792]{1,0:T(8,128)S(1)}, f32[512,1792]{1,0:T(8,128)}, u32[]{:S(2)}) copy-start(f32[512,1792]{1,0:T(8,128)} %param.3) | copy-start | bytes 11010052
  419.4 13.7 %copy-start.4 = (f32[1792,512]{1,0:T(8,128)S(1)}, f32[1792,512]{1,0:T(8,128)}, u32[]{:S(2)}) copy-start(f32[1792,512]{1,0:T(8,128)} %all-gather.4.cloned.1.call-done) | copy-start | bytes 11010052
Sparse Core Ops, SparseCore 0:
  17.7 89.6 all-reduce.2
  112.1 49.0 all-gather.5
  383.7 29.3 all-gather.3
where the time goes:
time: 459 us; the launch traced here: 454 us
  waiting for transfers between devices  139 us (30%)
  other arithmetic  132 us (29%)
  blocking collectives  79.5 us (17%)
  matrix products  70.5 us (15%)
  between operations  16.8 us (4%)
  local copies, waits for them, and re-layouts  15.9 us (3%)
    psum x1, waiting for transfers between devices, per_device(): left = lax.psum(partial_value, FSDP)  89.8 us
    another operation x14, other arithmetic, orthonormal(): lower = jnp.linalg.cholesky(gram)  79 us
    all_gather x1, waiting for transfers between devices, total_of_pieces(): parts = lax.all_gather(value, axis)  48.7 us
    all_to_all x1, blocking collectives, sum_at_owner(): lax.all_to_all(in_blocks(value, dim, devices), axis, 0, 0, tiled=True)  47.3 us
    another operation x3, other arithmetic, orthonormal(): return jax.scipy.linalg.solve_triangular(lower, block.T, lower=True).T  41.2 us
    psum x4, blocking collectives, over_axes(): return functools.reduce(lax.psum, axes, value)  32.2 us
    dot_general x2, matrix products, outer_rank(): lax.dot_general(first, second, (((1,), (1,)), ((), ())), precision=lax.Pr...  27.4 us
    dot_general x2, matrix products, inner_rows(): lax.dot_general(first, second, (((0,), (0,)), ((), ())), precision=lax.Pr...  16.8 us
  transfers between devices with their start and end apart: 3, of which 2 were waited for; matrix products, arithmetic and copies ran while one was open for 0% of the time, Pallas kernels for 0%

commit v1 on v0

--- a/solution.py
+++ b/solution.py
@@ -64,7 +64,8 @@
     partial_value = jnp.dot(
         buffer, right_factor, precision=lax.Precision.HIGHEST, preferred_element_type=jnp.float32
     )
-    left = lax.psum(partial_value, FSDP)
+    half = lax.psum(partial_value, "fsdp_1")
+    left = lax.psum(half, "fsdp_0")
     gram = total_of_pieces(inner_rows(left, left), TENSOR)
     ortho = orthonormal(left, gram)
     right_part = inner_rows(buffer, ortho)

time: 459 us -> 469 us (1.022)
  waiting for transfers between devices: 139 us -> 148 us
    psum x1 -> x2, waiting for transfers between devices: 89.8 us -> 98 us  [the longest x1 49.3 us: per_device(): left = lax.psum(half, 'fsdp_0')]
  transfers between devices with their start and end apart: 3 -> 4, of which waited for: 2 -> 3; matrix products, arithmetic and copies ran while one was open for 0% -> 0% of each run, Pallas kernels for 0% -> 0%
where the time goes in v1:
time: 469 us; the launch traced here: 464 us
  waiting for transfers between devices  148 us (32%)
  other arithmetic  132 us (28%)
  blocking collectives  79.5 us (17%)
  matrix products  70.5 us (15%)
  between operations  16.8 us (4%)
  local copies, waits for them, and re-layouts  15.9 us (3%)
    another operation x14, other arithmetic, orthonormal(): lower = jnp.linalg.cholesky(gram)  79 us
    all_gather x1, waiting for transfers between devices, total_of_pieces(): parts = lax.all_gather(value, axis)  50.4 us
    psum x1, waiting for transfers between devices, per_device(): left = lax.psum(half, 'fsdp_0')  49.3 us
    psum x1, waiting for transfers between devices, per_device(): half = lax.psum(partial_value, 'fsdp_1')  48.7 us
    all_to_all x1, blocking collectives, sum_at_owner(): lax.all_to_all(in_blocks(value, dim, devices), axis, 0, 0, tiled=True)  47.3 us
    another operation x3, other arithmetic, orthonormal(): return jax.scipy.linalg.solve_triangular(lower, block.T, lower=True).T  41.2 us
    psum x4, blocking collectives, over_axes(): return functools.reduce(lax.psum, axes, value)  32.2 us
    dot_general x2, matrix products, outer_rank(): lax.dot_general(first, second, (((1,), (1,)), ((), ())), precision=lax.Pr...  27.4 us
  transfers between devices with their start and end apart: 4, of which 3 were waited for; matrix products, arithmetic and copies ran while one was open for 0% of the time, Pallas kernels for 0%

profile of v1, /device:TPU:0, one launch (start us, length us, event | category | flops | bytes accessed | tf_op | source)
XLA Modules:
  0.0 463.6 jit_solution(1891172943867786301)
XLA Ops:
  7.2 10.3 %fusion.1 = f32[512,512]{1,0:T(8,128)} fusion(f32[1792,512]{1,0:T(8,128)} %param.5, f32[512,1792]{1,0:T(8,128)} %param.3, bf16[512,1792]{1,0:T(8,128)(2,1)} %param.4), kind=kOutput, calls=%fused_computation.7 | convolution fusion | flops 5638979584 | bytes 10223616 | tf_op jit(solution)/shard_map/dot_general | solution.py:64
  17.6 48.7 %all-reduce.4.cloned.1.call-done = f32[512,512]{1,0:T(8,128)} async-done(((f32[512,512]{1,0:T(8,128)}), f32[512,512]{1,0:T(8,128)}) %all-reduce.4.cloned.1.call-update) | async-done | bytes 1048592 | tf_op jit(solution)/shard_map/psum | solution.py:67
  66.4 49.3 %all-reduce.6.cloned.1.call-done = f32[512,512]{1,0:T(8,128)} async-done(((f32[512,512]{1,0:T(8,128)}), f32[512,512]{1,0:T(8,128)}) %all-reduce.6.cloned.1.call-update) | async-done | bytes 1048592 | tf_op jit(solution)/shard_map/psum | solution.py:68
  115.7 4.5 fusion.36
  120.8 50.4 %all-gather.6.cloned.1.call-done = f32[4096,512]{1,0:T(8,128)} async-done(((f32[512,512]{1,0:T(8,128)}), f32[4096,512]{1,0:T(8,128)}) %all-gather.6.cloned.1.call-update) | async-done | bytes 8388624 | tf_op jit(solution)/shard_map/all_gather | solution.py:17
  171.2 4.5 reduce_sum.27
  176.3 1.0 copy-done.8
  177.3 11.7 %cholesky.104 = f32[128,128]{1,0:T(8,128)S(1)} custom-call(f32[128,128]{1,0:T(8,128)S(1)} %cholesky.266), custom_call_target="Cholesky" | custom-call | tf_op jit(solution)/shard_map/jit(cholesky)/cholesky | solution.py:58
  189.1 9.8 %custom-call.31 = f32[1,128,128]{1,2,0:T(8,128)S(1)} custom-call(f32[1,128,128]{2,1,0:T(8,128)S(1)} %get-tuple-element.30), custom_call_target="InvertDiagBlocksLowerTriangular" | custom-call | tf_op jit(solution)/shard_map/jit(cholesky)/cholesky | solution.py:58
  199.0 1.2 constant_dynamic-update-slice_fusion.3
  200.2 1.3 convolution_subtract_fusion.3
  201.5 11.9 %cholesky.217 = f32[128,128]{1,0:T(8,128)S(1)} custom-call(f32[128,128]{1,0:T(8,128)S(1)} %cholesky.270), custom_call_target="Cholesky" | custom-call | tf_op jit(solution)/shard_map/jit(cholesky)/cholesky | solution.py:58
  213.4 9.8 %custom-call.32 = f32[1,128,128]{1,2,0:T(8,128)S(1)} custom-call(f32[1,128,128]{2,1,0:T(8,128)S(1)} %get-tuple-element.27), custom_call_target="InvertDiagBlocksLowerTriangular" | custom-call | tf_op jit(solution)/shard_map/jit(cholesky)/cholesky | solution.py:58
  223.5 1.3 convolution_subtract_fusion.4
  224.8 11.7 %cholesky.238 = f32[128,128]{1,0:T(8,128)S(1)} custom-call(f32[128,128]{1,0:T(8,128)S(1)} %cholesky.275), custom_call_target="Cholesky" | custom-call | tf_op jit(solution)/shard_map/jit(cholesky)/cholesky | solution.py:58
  236.5 0.7 compare_reduce_fusion.1
  237.2 9.8 %custom-call.33 = f32[1,128,128]{1,2,0:T(8,128)S(1)} custom-call(f32[1,128,128]{2,1,0:T(8,128)S(1)} %get-tuple-element.24), custom_call_target="InvertDiagBlocksLowerTriangular" | custom-call | tf_op jit(solution)/shard_map/jit(cholesky)/cholesky | solution.py:58
  247.3 1.2 convolution_subtract_fusion.5
  248.5 12.1 %cholesky.255 = f32[128,128]{1,0:T(8,128)S(1)} custom-call(f32[128,128]{1,0:T(8,128)S(1)} %convolution_subtract_fusion.5), custom_call_target="Cholesky" | custom-call | tf_op jit(solution)/shard_map/jit(cholesky)/cholesky | solution.py:58
  260.6 0.6 compare_reduce_fusion
  261.3 0.7 compare_reduce_fusion.2
  264.5 1.1 select_select_fusion
  265.6 14.2 %while.1 = (s32[]{:T(128)}, f32[512,512]{1,0:T(8,128)}, s32[4,2]{0,1:T(2,128)S(1)}, f32[4,128,128]{2,1,0:T(8,128)}, s32[]{:T(128)}) while((s32[]{:T(128)}, f32[512,512]{1,0:T(8,128)}, s32[4,2]{0,1:T(2,128)S(1)}, f32[4,128,128]{2,1,0:T(8,128)}, s32[]{:T(128)}) %tuple.31), condition=%wide.while_cond, body=%wide.while_body.sunk | while | flops 2 | bytes 132205 | solution.py:59
  265.6 0.6 fusion.48
  266.3 2.9 bitcast_dynamic-update-slice_fusion.2
  269.2 0.6 fusion.48
  269.8 2.9 bitcast_dynamic-update-slice_fusion.2
  272.8 0.6 fusion.48
  273.4 2.9 bitcast_dynamic-update-slice_fusion.2
  276.9 2.8 bitcast_dynamic-update-slice_fusion.2
  279.7 40.1 %custom-call.34 = f32[4,128,128]{1,2,0:T(8,128)S(1)} custom-call(f32[4,128,128]{2,1,0:T(8,128)} %get-tuple-element.10), custom_call_target="InvertDiagBlocksLowerTriangular" | custom-call | tf_op jit(solution)/shard_map/jit(_solve_triangular)/triangular_solve | solution.py:59
  320.6 1.9 convolution_subtract_fusion.1
  322.4 1.3 fusion.24
  323.7 1.9 convolution_subtract_fusion
  325.6 1.3 fusion.22
  326.9 2.5 convolution_subtract_fusion.2
  329.4 1.3 fusion.21
  330.7 12.3 %fusion = f32[1792,512]{1,0:T(8,128)S(1)} fusion(f32[512,1792]{1,0:T(8,128)S(1)} %copy-done, bf16[512,1792]{1,0:T(8,128)(2,1)S(1)} %copy-done.2, f32[128,512]{1,0:T(8,128)S(1)} %fusion.21, f32[128,512]{1,0:T(8,128)S(1)} %fusion.22, f32[128,512]{1,0:T(8,128)S(1)} %fusion.24, f32[128,512]{1,0:T(8,128)S(1)} %fusion.11), kind=kOutput, calls=%fused_computation.6 | convolution fusion | flops 5639766016 | bytes 10223616 | tf_op jit(solution)/shard_map/dot_general | solution.py:38
  343.0 47.3 %all_to_all.5 = f32[8,224,512]{2,1,0:T(8,128)} all-to-all(f32[8,224,512]{2,1,0:T(8,128)S(1)} %bitcast.56), channel_id=1, replica_groups=mesh['tensor_0'=4,'tensor_1'=2,'fsdp_0'=4,'fsdp_1'=4] {'tensor_0','tenso..., dimensions={0} | all-to-all | bytes 7340032 | tf_op jit(solution)/shard_map/all_to_all | solution.py:29
  390.3 3.3 reduce_sum.28
  393.5 1.1 multiply_reduce_fusion
  394.6 8.9 %psum.44 = f32[512]{0:T(512)S(1)} all-reduce(f32[512]{0:T(512)S(1)} %multiply_reduce_fusion), channel_id=1, replica_groups=mesh['tensor_0'=4,'tensor_1'=2,'fsdp_0'=4,'fsdp_1'=4] {'tensor_0'}, use_global_device_ids=true, to_apply=%region_13.14 | all-reduce | flops 512 | bytes 4096 | tf_op jit(solution)/shard_map/psum | solution.py:34
  403.5 2.5 psum.45
  406.0 10.4 %psum.46 = f32[512]{0:T(512)S(1)} all-reduce(f32[512]{0:T(512)S(1)} %psum.45), channel_id=1, replica_groups=mesh['tensor_0'=4,'tensor_1'=2,'fsdp_0'=4,'fsdp_1'=4] {'fsdp_0'}, use_global_device_ids=true, to_apply=%region_15.16 | all-reduce | flops 512 | bytes 4096 | tf_op jit(solution)/shard_map/psum | solution.py:34
  416.4 10.5 %psum.47 = f32[512]{0:T(512)S(1)} all-reduce(f32[512]{0:T(512)S(1)} %psum.46), channel_id=1, replica_groups=mesh['tensor_0'=4,'tensor_1'=2,'fsdp_0'=4,'fsdp_1'=4] {'fsdp_1'}, use_global_device_ids=true, to_apply=%region_16.17 | all-reduce | flops 512 | bytes 4096 | tf_op jit(solution)/shard_map/psum | solution.py:34
  426.9 2.5 broadcast_divide_fusion
  429.4 13.7 %convolution_multiply_fusion = f32[512,1792]{1,0:T(8,128)} fusion(f32[1792,512]{1,0:T(8,128)S(1)} %broadcast_divide_fusion, f32[128,512]{1,0:T(8,128)S(1)} %fusion.21, f32[128,512]{1,0:T(8,128)S(1)} %copy-done.7, f32[128,512]{1,0:T(8,128)S(1)} %fusion.24, f32[128,512]{1,0:T(8,128)S(1)} %fusion.11), kind=kOutput, calls=%fused_computation.4 | convolution fusion | flops 5638848512 | bytes 8388608 | tf_op jit(solution)/shard_map/dot_general | solution.py:48
  443.2 13.7 %multiply_subtract_fusion = f32[512,1792]{1,0:T(8,128)} fusion(f32[1792,512]{1,0:T(8,128)S(1)} %copy-done.4, f32[512,1792]{1,0:T(8,128)S(1)} %copy-done.1, bf16[512,1792]{1,0:T(8,128)(2,1)S(1)} %copy-done.2, f32[128,512]{1,0:T(8,128)S(1)} %fusion.21, f32[128,512]{1,0:T(8,128)S(1)} %copy-done.7, f32[128,512]{1,0:T(8,128)S(1)} %fusion.24, ...), kind=kOutput, calls=%fused_computation.2 | convolution fusion | flops 5641601024 | bytes 13893632 | tf_op jit(solution)/shard_map/dot_general | solution.py:48
  (50 shorter events, 3.6 us)
Async XLA Ops:
  7.2 59.2 %all-reduce.4.cloned.1.call-start = ((), (), s32[]{:S(2)}) async-start(), calls=%async_computation.1 | async-start | bytes 2097152 | tf_op jit(solution)/shard_map/psum | solution.py:67
  17.6 98.1 %all-reduce.6.cloned.1.call-start = ((), (), s32[]{:S(2)}) async-start(), calls=%async_computation.2 | async-start | bytes 2097152 | tf_op jit(solution)/shard_map/psum | solution.py:68
  66.4 104.9 %all-gather.6.cloned.1.call-start = ((), (), s32[]{:S(2)}) async-start(), calls=%async_computation.4 | async-start | bytes 9437184 | tf_op jit(solution)/shard_map/all_gather | solution.py:17
  120.2 306.6 %all-gather.4.cloned.1.call-start = ((), (), s32[]{:S(2)}) async-start(), calls=%async_computation.3 | async-start | bytes 4128768 | tf_op jit(solution)/shard_map/all_gather | solution.py:74
  176.3 1.0 copy-start.8
  189.0 130.9 %copy-start.5 = (f32[512,512]{1,0:T(8,128)S(1)}, f32[512,512]{1,0:T(8,128)}, u32[]{:S(2)}) copy-start(f32[512,512]{1,0:T(8,128)} %all-reduce.6.cloned.1.call-done) | copy-start | bytes 3145732
  265.6 65.1 %copy-start.2 = (bf16[512,1792]{1,0:T(8,128)(2,1)S(1)}, bf16[512,1792]{1,0:T(8,128)(2,1)}, u32[]{:S(2)}) copy-start(bf16[512,1792]{1,0:T(8,128)(2,1)} %param.4) | copy-start | bytes 5505028
  319.9 0.7 copy-start.9
  319.9 10.8 %copy-start = (f32[512,1792]{1,0:T(8,128)S(1)}, f32[512,1792]{1,0:T(8,128)}, u32[]{:S(2)}) copy-start(f32[512,1792]{1,0:T(8,128)} %param.3) | copy-start | bytes 11010052
  326.9 16.1 %copy-start.6 = (f32[128,512]{1,0:T(8,128)}, f32[128,512]{1,0:T(8,128)S(1)}, u32[]{:S(2)}) copy-start(f32[128,512]{1,0:T(8,128)S(1)} %fusion.22) | copy-start | bytes 786436
  426.8 2.6 copy-start.7
  429.4 13.7 %copy-start.3 = (f32[1792,512]{1,0:T(8,128)}, f32[1792,512]{1,0:T(8,128)S(1)}, u32[]{:S(2)}) copy-start(f32[1792,512]{1,0:T(8,128)S(1)} %broadcast_divide_fusion) | copy-start | bytes 11010052
  429.4 13.7 %copy-start.1 = (f32[512,1792]{1,0:T(8,128)S(1)}, f32[512,1792]{1,0:T(8,128)}, u32[]{:S(2)}) copy-start(f32[512,1792]{1,0:T(8,128)} %param.3) | copy-start | bytes 11010052
  429.4 13.7 %copy-start.4 = (f32[1792,512]{1,0:T(8,128)S(1)}, f32[1792,512]{1,0:T(8,128)}, u32[]{:S(2)}) copy-start(f32[1792,512]{1,0:T(8,128)} %all-gather.4.cloned.1.call-done) | copy-start | bytes 11010052
Sparse Core Ops, SparseCore 0:
  17.7 48.5 all-reduce.3
  68.7 46.9 all-reduce.5
  120.4 50.8 all-gather.5
  393.7 29.3 all-gather.3
